TPU v7x, 128 devices: a whole 4x4x4 slice. The times are simulated.
128 devices in a mesh: row: 8 (over z, core), col: 16 (over y, x).
Axes of the slice: x: 4, y: 4, z: 4, core: 2. Of those that a mesh axis runs over, the one named last changes fastest.
Arguments:
- inverse: bfloat16 [18432, 18432], P('row', 'col'), may hold values from -0.046875 to 0.046875
- pair_block: bfloat16 [18432, 2560], P('row', 'col'), may hold values from -6 to 6
- coeffs: bfloat16 [5120, 2560], P('row'), may hold values from -0.125 to 0.125
Outputs:
- gradient_ao: bfloat16 [18432, 5120], P('col', 'row')
All inputs are finite; a program needn't handle non-finite values.
Results may differ from a plain program's by a relative error of at most 0.0049.
Values may be sent and summed in bfloat16 or wider, within the bound.
A program may use at most 128 MiB of HBM per device.

v0:
```python
import jax
import jax.numpy as jnp
from jax import lax
from jax.sharding import PartitionSpec as P


def shards(inverse, pair_block, coeffs):
    cols_here = inverse.shape[1]
    row_count = lax.axis_size("row")
    col_count = lax.axis_size("col")
    blocks_per = col_count // row_count
    col_index = lax.axis_index("col")
    row_index = lax.axis_index("row")
    offset_rows = col_index % blocks_per * cols_here
    holds_diag = col_index // blocks_per == row_index
    columns = lax.all_gather(pair_block, "col", axis=1, tiled=True)
    product = lax.dot_general(
        inverse, columns, (((0,), (0,)), ((), ())), preferred_element_type=jnp.float32
    )
    diagonal = lax.dynamic_slice_in_dim(columns, offset_rows, cols_here, 0).astype(jnp.float32)
    partial_value = product - jnp.where(holds_diag, diagonal, jnp.zeros_like(diagonal))
    portion = lax.psum_scatter(partial_value, "row", scatter_dimension=1, tiled=True)
    gamma_aux = lax.all_gather(portion.astype(jnp.bfloat16), "row", axis=1, tiled=True)
    result = lax.dot_general(
        gamma_aux, coeffs, (((1,), (1,)), ((), ())), preferred_element_type=jnp.float32
    )
    return result.astype(jnp.bfloat16)


def solution(mesh):
    placed = (P("row", "col"), P("row", "col"), P("row", None))
    return jax.shard_map(
        shards, mesh=mesh, in_specs=placed, out_specs=P("col", "row"), check_vma=False
    )
```

profile of v0, /device:TPU:1, one launch (start us, length us, event | category | flops | bytes accessed | tf_op | source)
XLA Modules:
  0.0 247.1 jit_solution(13387108250398124115)
XLA Ops:
  6.5 0.0 copy-start
  6.5 0.0 all-gather.3.cloned.1.call-start
  6.5 0.7 all-gather.3.cloned.1.call-update
  7.3 0.0 reduce-scatter.2.cloned.1.call-start
  7.3 91.7 %all-gather.3.cloned.1.call-done = bf16[2304,2560]{0,1:T(8,128)(2,1)} async-done(((bf16[2304,160]{0,1:T(8,128)(2,1)}), bf16[2304,2560]{0,1:T(8,128)(2,1)}) %all-gather.3.cloned.1.call-update) | async-done | bytes 11796496 | tf_op jit(solution)/shard_map/all_gather | solution.py:16
  99.0 22.4 %convolution_subtract_fusion = f32[1152,2560]{0,1:T(8,128)} fusion(bf16[2304,2560]{0,1:T(8,128)(2,1)} %all-gather.3.cloned.1.call-done, bf16[2304,1152]{1,0:T(8,128)(2,1)} %param.3, s32[]{:T(128)S(6)} %select_n.25, pred[]{:T(512)S(6)} %eq.5), kind=kOutput, calls=%fused_computation | convolution fusion | flops 13598392320 | bytes 34799620 | tf_op jit(solution)/shard_map/dot_general | solution.py:17
  121.4 0.0 reduce-scatter.2.cloned.1.call-update
  121.4 0.0 all-gather.5.cloned.1.call-start
  121.5 68.0 %reduce-scatter.2.cloned.1.call-done = f32[1152,320]{0,1:T(8,128)} async-done(((f32[1152,2560]{0,1:T(8,128)}), f32[1152,320]{0,1:T(8,128)}) %reduce-scatter.2.cloned.1.call-update) | async-done | bytes 1474576 | tf_op jit(solution)/shard_map/reduce_scatter | solution.py:22
  189.5 2.3 convert_element_type.10
  191.8 0.0 all-gather.5.cloned.1.call-update
  191.8 40.2 %all-gather.5.cloned.1.call-done = bf16[1152,2560]{0,1:T(8,128)(2,1)} async-done(((bf16[1152,320]{0,1:T(8,128)(2,1)}), bf16[1152,2560]{0,1:T(8,128)(2,1)}) %all-gather.5.cloned.1.call-update) | async-done | bytes 5898256 | tf_op jit(solution)/shard_map/all_gather | solution.py:23
  232.0 0.0 copy-done
  232.0 8.6 %convolution_convert_fusion = bf16[1152,640]{1,0:T(8,128)(2,1)} fusion(bf16[1152,2560]{0,1:T(8,128)(2,1)} %all-gather.5.cloned.1.call-done, bf16[640,2560]{1,0:T(8,128)(2,1)S(1)} %copy-done), kind=kOutput, calls=%fused_computation.1 | convolution fusion | flops 3775610880 | bytes 10649600 | tf_op jit(solution)/shard_map/dot_general | solution.py:24
Async XLA Ops:
  6.5 225.5 %copy-start = (bf16[640,2560]{1,0:T(8,128)(2,1)S(1)}, bf16[640,2560]{1,0:T(8,128)(2,1)}, u32[]{:S(2)}) copy-start(bf16[640,2560]{1,0:T(8,128)(2,1)} %param.5) | copy-start | bytes 9830404
  6.5 92.5 %all-gather.3.cloned.1.call-start = ((), (), s32[]{:S(2)}) async-start(), calls=%async_computation.1 | async-start | bytes 12533760 | tf_op jit(solution)/shard_map/all_gather | solution.py:16
  7.3 182.2 %reduce-scatter.2.cloned.1.call-start = ((), (), s32[]{:S(2)}) async-start(), calls=%async_computation.2 | async-start | bytes 13271040 | tf_op jit(solution)/shard_map/reduce_scatter | solution.py:22
  121.4 110.6 %all-gather.5.cloned.1.call-start = ((), (), s32[]{:S(2)}) async-start(), calls=%async_computation.3 | async-start | bytes 6635520 | tf_op jit(solution)/shard_map/all_gather | solution.py:23
Sparse Core Ops, SparseCore 0:
  9.5 89.5 all-gather.2
  121.6 67.8 reduce-scatter.1
  191.9 40.0 all-gather.4
where the time goes:
time: 247 us
  waiting for transfers between devices  201 us (81%)
  matrix products  31 us (13%)
  between operations  13.1 us (5%)
    all_gather x1, waiting for transfers between devices, shards(): columns = lax.all_gather(pair_block, 'col', axis=1, tiled=True)  91.7 us
    reduce_scatter x1, waiting for transfers between devices, shards(): lax.psum_scatter(partial_value, 'row', scatter_dimension=1, tiled=True)  68 us
    all_gather x1, waiting for transfers between devices, shards(): lax.all_gather(portion.astype(jnp.bfloat16), 'row', axis=1, tiled=True)  40.2 us
    dot_general x1, matrix products, shards(): lax.dot_general(inverse, columns, (((0,), (0,)), ((), ())), preferred_ele...  22.4 us
    dot_general x1, matrix products, shards(): lax.dot_general(gamma_aux, coeffs, (((1,), (1,)), ((), ())), preferred_el...  8.58 us
  transfers between devices with their start and end apart: 3, of which 3 were waited for; matrix products, arithmetic and copies ran while one was open for 0% of the time, Pallas kernels for 0%

commit v1 on v0

v1 whole, which is shorter than its diff:
```python
import jax
import jax.numpy as jnp
from jax import lax
from jax.experimental import pallas as pl
from jax.experimental.pallas import tpu as pltpu
from jax.sharding import PartitionSpec as P

MESH = pl.DeviceIdType.MESH
F32, BF16 = jnp.float32, jnp.bfloat16

SLOTS = [
    (0, 0, 0), (1, 0, 0),
    (0, 3, 0), (0, 1, 0), (1, 0, 3), (1, 0, 1),
    (0, 0, 3), (0, 0, 1), (1, 3, 0), (1, 1, 0),
    (0, 2, 0), (1, 0, 2),
    (0, 3, 3), (0, 3, 1), (1, 3, 3), (1, 1, 3),
    (0, 1, 3), (0, 1, 1), (1, 3, 1), (1, 1, 1),
    (0, 0, 2), (1, 2, 0),
    (0, 2, 3), (0, 2, 1), (1, 3, 2), (1, 1, 2),
    (0, 3, 2), (1, 2, 3),
    (0, 1, 2), (1, 2, 1),
    (0, 2, 2), (1, 2, 2),
]
SLOT_OF = {key: at for at, key in enumerate(SLOTS)}


def routes():
    sends, parts = {}, {}

    def add(half, first, second, step_first, step_second, part):
        def key(a, b):
            return (half, a % 4, b % 4) if half == 0 else (half, b % 4, a % 4)

        source = SLOT_OF[key(first, second)]
        target = SLOT_OF[key(first - step_first, second - step_second)]
        step = (step_first, step_second) if half == 0 else (step_second, step_first)
        copy = (source, target, part) + step
        sends.setdefault(source, []).append(copy)
        parts.setdefault(target, []).append(copy)

    for half in (0, 1):
        for step in (1, -1):
            add(half, 0, 0, step, 0, "all")
        add(half, -1, 0, 1, 0, "low")
        add(half, 1, 0, -1, 0, "high")
        for first in (0, -1, 1, 2):
            for step in (1, -1):
                add(half, first, 0, 0, step, "all")
            add(half, first, -1, 0, 1, "low" if first in (0, 1) else "lower")
            add(half, first, 1, 0, -1, "high" if first in (0, 1) else "higher")
    return sends, parts


SENDS, PARTS = routes()
COPIES = sorted({copy for group in SENDS.values() for copy in group}, key=lambda c: (c[1], c[2]))
COPY_ID = {copy: at for at, copy in enumerate(COPIES)}

TICK = 128
LAG2, LAG3, LAG4, LAG5 = 1, 3, 5, 6


def kernel(inv_hbm, pair_hbm, coef_hbm, out_ref, inv, pair, cstage, ct, cts, part, crecv, zsend, keep, zrecv, gamma, acc,
           local, pair_s, pair_r, core_s, core_r, z_s, z_r, ag_s, ag_r, back_s, back_r):
    rows, here = pair_hbm.shape
    cols = inv_hbm.shape[1]
    basis, virt = coef_hbm.shape
    hb = rows // 2
    ticks = virt // TICK
    half_tick, piece = TICK // 2, TICK // 8
    row, col = lax.axis_index("row"), lax.axis_index("col")
    z, core = row // 2, row % 2
    y, x = col // 4, col % 4

    def at_xy(step_x, step_y):
        return (row, (y + step_y) % 4 * 4 + (x + step_x) % 4)

    def at_z(step):
        return ((z + step) % 4 * 2 + core, col)

    sibling = (z * 2 + 1 - core, col)

    def ds(start, size):
        return pl.ds(pl.multiple_of(start, size), size)

    load_pair = pltpu.make_async_copy(pair_hbm, pair.at[pl.ds(0, rows)], local.at[0])
    load_inv = pltpu.make_async_copy(inv_hbm, inv, local.at[1])
    quarter = virt // 4
    load_c = [
        pltpu.make_async_copy(coef_hbm.at[:, pl.ds(k * quarter, quarter)], cstage.at[k % 2], local.at[2 + k]) for k in range(4)
    ]
    load_pair.start()
    load_c[0].start()
    load_c[1].start()
    load_inv.start()

    barrier = pltpu.get_barrier_semaphore()
    for device in (at_xy(1, 0), at_xy(3, 0), at_xy(0, 1), at_xy(0, 3), at_z(1), at_z(2), at_z(3), sibling):
        pl.semaphore_signal(barrier, inc=1, device_id=device, device_id_type=MESH)
    pl.semaphore_wait(barrier, 8)

    def pair_copy(copy):
        source, target, span, step_x, step_y = copy
        start, size = {"all": (0, 80), "low": (0, 48), "high": (48, 32), "lower": (0, 32), "higher": (32, 48)}[span]
        at = COPY_ID[copy]
        return pltpu.make_async_remote_copy(
            pair.at[pl.ds(source * hb + start, size)], pair.at[pl.ds(target * hb + start, size)], pair_s.at[at], pair_r.at[at],
            device_id=at_xy(step_x, step_y), device_id_type=MESH,
        )

    load_pair.wait()
    own = sorted(SENDS[0] + SENDS[1], key=lambda c: (c[3] != 0) != (c[0] == 0))
    for copy in own:
        pair_copy(copy).start()

    acc[...] = jnp.zeros_like(acc)
    for k in range(4):
        load_c[k].wait()
        ct[pl.ds(k * quarter, quarter), :] = cstage[k % 2].T
        if k + 2 < 4:
            load_c[k + 2].start()
    for slot, (half, dx, dy) in enumerate(SLOTS):
        block = (y + dy) % 4 * 4 + (x + dx) % 4
        start = pl.multiple_of(block * rows + half * hb, hb)
        cts[pl.ds(slot * hb, hb), :] = ct[pl.ds(start, hb), :]
    load_inv.wait()

    holds_diag = col // 2 == row
    diag_at = pl.multiple_of(col % 2 * cols, cols)

    def core_copy(u):
        return pltpu.make_async_remote_copy(
            part.at[u % 4, ds((1 - core) * half_tick, half_tick)], crecv.at[ds(u * half_tick, half_tick)],
            core_s.at[u], core_r.at[u], device_id=sibling, device_id_type=MESH,
        )

    def z_copy(u, step):
        return pltpu.make_async_remote_copy(
            zsend.at[ds(u * half_tick + (z + step) % 4 * piece, piece)], zrecv.at[ds((u * 3 + step - 1) * piece, piece)],
            z_s.at[u, step - 1], z_r.at[u, step - 1], device_id=at_z(step), device_id_type=MESH,
        )

    def spread_copy(u, step):
        mine = ds(u * TICK + core * half_tick + z * piece, piece)
        return pltpu.make_async_remote_copy(
            gamma.at[mine], gamma.at[mine], ag_s.at[u, step - 1], ag_r.at[u, step - 1],
            device_id=at_z(step), device_id_type=MESH,
        )

    def back_copy(u):
        mine = ds(u * TICK + core * half_tick, half_tick)
        return pltpu.make_async_remote_copy(
            gamma.at[mine], gamma.at[mine], back_s.at[u], back_r.at[u], device_id=sibling, device_id_type=MESH,
        )

    def product(t):
        for k in range(ticks):
            slots = [s for s in range(2, 32) if s * hb // TICK == k]
            if slots:
                @pl.when(t == k)
                def _():
                    for slot in slots:
                        for copy in PARTS[slot]:
                            pair_copy(copy).wait_recv()
                        for copy in SENDS.get(slot, ()):
                            pair_copy(copy).start()

        @pl.when(t >= 4)
        def _():
            core_copy(t - 4).wait_send()

        now = ds(t * TICK, TICK)
        part[t % 4] = jnp.dot(pair[now, :], inv[...], preferred_element_type=F32)

        @pl.when(holds_diag)
        def _():
            part[t % 4] = part[t % 4] - pair[now, pl.ds(diag_at, cols)].astype(F32)

        core_copy(t).start()

    def add_cores(u):
        core_copy(u).wait_recv()
        total = part[u % 4, ds(core * half_tick, half_tick)] + crecv[ds(u * half_tick, half_tick)]
        zsend[ds(u * half_tick, half_tick)] = total.astype(BF16)
        keep[u % 4] = (
            part[u % 4, ds(core * half_tick + z * piece, piece)] + crecv[ds(u * half_tick + z * piece, piece)]
        )
        for step in (2, 1, 3):
            z_copy(u, step).start()

    def add_z(u):
        for step in (1, 2, 3):
            z_copy(u, step).wait_recv()
        total = keep[u % 4]
        for step in (1, 2, 3):
            total = total + zrecv[ds((u * 3 + step - 1) * piece, piece)].astype(F32)
        gamma[ds(u * TICK + core * half_tick + z * piece, piece)] = total.astype(BF16)
        for step in (2, 1, 3):
            spread_copy(u, step).start()

    def spread_cores(u):
        for step in (1, 2, 3):
            spread_copy(u, step).wait_recv()
        back_copy(u).start()
        for step in (1, 2, 3):
            z_copy(u, step).wait_send()

    def transform(u):
        back_copy(u).wait_recv()
        now = ds(u * TICK, TICK)
        acc[...] += lax.dot_general(gamma[now, :], cts[now, :], (((0,), (0,)), ((), ())), preferred_element_type=F32)
        for step in (1, 2, 3):
            spread_copy(u, step).wait_send()
        back_copy(u).wait_send()

    def tick(t, _):
        for lag, stage in ((LAG2, add_cores), (LAG3, add_z), (LAG4, spread_cores), (0, product), (LAG5, transform)):
            @pl.when((t >= lag) & (t < ticks + lag))
            def _():
                stage(t - lag)
        return 0

    lax.fori_loop(0, ticks + LAG5, tick, 0)
    out_ref[...] = acc[...].astype(BF16)
    for copy in COPIES:
        pair_copy(copy).wait_send()
    for u in range(ticks - 4, ticks):
        core_copy(u).wait_send()


def shards(inverse, pair_block, coeffs):
    here, cols = inverse.shape
    rows = pair_block.shape[1]
    basis, virt = coeffs.shape
    ticks = virt // TICK
    dma = pltpu.SemaphoreType.DMA
    any_space = pl.BlockSpec(memory_space=pl.ANY)
    return pl.pallas_call(
        kernel,
        out_shape=jax.ShapeDtypeStruct((cols, basis), BF16),
        in_specs=[any_space] * 3,
        out_specs=pl.BlockSpec(memory_space=pltpu.VMEM),
        scratch_shapes=[
            pltpu.VMEM((here, cols), BF16),
            pltpu.VMEM((virt, here), BF16),
            pltpu.VMEM((2, basis, virt // 4), BF16),
            pltpu.VMEM((virt, basis), BF16),
            pltpu.VMEM((virt, basis), BF16),
            pltpu.VMEM((4, TICK, cols), F32),
            pltpu.VMEM((virt // 2, cols), F32),
            pltpu.VMEM((virt // 2, cols), BF16),
            pltpu.VMEM((4, TICK // 8, cols), F32),
            pltpu.VMEM((ticks * 3 * TICK // 8, cols), BF16),
            pltpu.VMEM((virt, cols), BF16),
            pltpu.VMEM((cols, basis), F32),
            dma((6,)),
            dma((len(COPIES),)), dma((len(COPIES),)),
            dma((ticks,)), dma((ticks,)),
            dma((ticks, 3)), dma((ticks, 3)),
            dma((ticks, 3)), dma((ticks, 3)),
            dma((ticks,)), dma((ticks,)),
        ],
        compiler_params=pltpu.CompilerParams(collective_id=0, has_side_effects=True, vmem_limit_bytes=60 << 20),
    )(inverse, pair_block.T, coeffs)


def solution(mesh):
    placed = (P("row", "col"), P("row", "col"), P("row", None))
    return jax.shard_map(
        shards, mesh=mesh, in_specs=placed, out_specs=P("col", "row"), check_vma=False
    )
```

time: 247 us -> 109 us (0.44)
  waiting for transfers between devices: 201 us -> 0 us
  Pallas kernels: 0 us -> 106 us
  matrix products: 31 us -> 0 us
  between operations: 13.1 us -> 0.01 us
  local copies, waits for them, and re-layouts: 0.01 us -> 2.61 us
    all_gather x2 -> x0, waiting for transfers between devices: 132 us -> none  [the longest x1 91.7 us: shards(): columns = lax.all_gather(pair_block, 'col', axis=1, tiled=True)]
    pallas_call x0 -> x1, Pallas kernels: none -> 106 us  [shards(): pl.pallas_call(kernel, out_shape=jax.ShapeDtypeStruct((cols, basis), BF16...]
    reduce_scatter x1 -> x0, waiting for transfers between devices: 68 us -> none  [shards(): lax.psum_scatter(partial_value, 'row', scatter_dimension=1, tiled=True)]
    dot_general x2 -> x0, matrix products: 31 us -> none  [the longest x1 22.4 us: shards(): lax.dot_general(inverse, columns, (((0,), (0,)), ((), ())), preferred_ele...]
    unnamed x2 -> x1, local copies, waits for them, and re-layouts: 0.01 us -> 2.61 us
  transfers between devices with their start and end apart: 3 -> 0, of which waited for: 3 -> 0; matrix products, arithmetic and copies ran while one was open for 0% -> 0% of each run, Pallas kernels for 0% -> 0%
where the time goes in v1:
time: 109 us
  Pallas kernels  106 us (97%)
  local copies, waits for them, and re-layouts  2.61 us (2%)
    pallas_call x1, Pallas kernels, shards(): pl.pallas_call(kernel, out_shape=jax.ShapeDtypeStruct((cols, basis), BF16...  106 us
    unnamed x1, local copies, waits for them, and re-layouts  2.61 us

profile of v1, /device:TPU:1, one launch (start us, length us, event | category | flops | bytes accessed | tf_op | source)
XLA Modules:
  0.0 108.6 jit_solution(16648703911891632028)
XLA Ops:
  0.0 106.0 %shard_map.37 = bf16[1152,640]{1,0:T(8,128)(2,1)} custom-call(bf16[2304,1152]{1,0:T(8,128)(2,1)} %inv_hbm.1, bf16[160,2304]{1,0:T(8,128)(2,1)} %bitcast.1, bf16[640,2560]{1,0:T(8,128)(2,1)} %coef_hbm.1), custom_call_target="tpu_custom_call" | custom-call | tf_op jit(solution)/shard_map/pallas_call | solution.py:237
  106.0 2.6 %copy.5 = bf16[1152,640]{1,0:T(8,128)(2,1)} copy(bf16[1152,640]{1,0:T(8,128)(2,1)} %shard_map.37) | data formatting | bytes 2949120

commit v2 on v1

v2 whole, which is shorter than its diff:
```python
import jax
import jax.numpy as jnp
from jax import lax
from jax.experimental import pallas as pl
from jax.experimental.pallas import tpu as pltpu
from jax.sharding import PartitionSpec as P

MESH = pl.DeviceIdType.MESH
F32, BF16 = jnp.float32, jnp.bfloat16

PARTS = ((0, 48), (48, 32))
HALF = 80
ARRIVALS = [
    (True, [(0, 3, 0), (0, 1, 0), (1, 0, 3), (1, 0, 1)]),
    (True, [(0, 0, 3), (0, 0, 1), (1, 3, 0), (1, 1, 0)]),
    (False, [(0, 2, 0), (1, 0, 2)]),
    (True, [(0, 3, 3), (0, 3, 1), (1, 3, 3), (1, 1, 3)]),
    (True, [(0, 1, 3), (0, 1, 1), (1, 3, 1), (1, 1, 1)]),
    (False, [(0, 0, 2), (1, 2, 0)]),
    (True, [(0, 2, 3), (0, 2, 1), (1, 3, 2), (1, 1, 2)]),
    (False, [(0, 3, 2), (1, 2, 3)]),
    (False, [(0, 1, 2), (1, 2, 1)]),
    (False, [(0, 2, 2), (1, 2, 2)]),
]


def slots():
    order = [(half, 0, 0, part) for half in (0, 1) for part in (0, 1)]
    groups = []
    for whole, blocks in ARRIVALS:
        for parts in ((0,), (1,)) if whole else ((0, 1),):
            first = len(order)
            order += [block + (part,) for part in parts for block in blocks]
            groups.append(range(first, len(order)))
    return order, groups


SLOTS, GROUPS = slots()
SLOT_OF = {key: at for at, key in enumerate(SLOTS)}
SIZES = [PARTS[key[3]][1] for key in SLOTS]
STARTS = [sum(SIZES[:at]) for at in range(len(SIZES))]


def routes():
    sends, filled = {}, {}

    def add(half, first, second, step_first, step_second, parts):
        def key(a, b, part):
            return (half, a % 4, b % 4, part) if half == 0 else (half, b % 4, a % 4, part)

        step = (step_first, step_second) if half == 0 else (step_second, step_first)
        for part in parts:
            source = SLOT_OF[key(first, second, part)]
            target = SLOT_OF[key(first - step_first, second - step_second, part)]
            copy = (source, target) + step
            sends.setdefault(source, []).append(copy)
            filled[target] = copy

    for half in (0, 1):
        for step in (1, -1):
            add(half, 0, 0, step, 0, (0, 1))
        add(half, -1, 0, 1, 0, (0,))
        add(half, 1, 0, -1, 0, (1,))
        for first in (0, -1, 1, 2):
            for step in (1, -1):
                add(half, first, 0, 0, step, (0, 1))
            part = 0 if first in (0, 1) else 1
            add(half, first, -1, 0, 1, (part,))
            add(half, first, 1, 0, -1, (1 - part,))
    return sends, filled


SENDS, FILLED = routes()
COPIES = [FILLED[slot] for slot in sorted(FILLED)]

TICK = 128
DIRECT = 4
RELAY_LAGS = (1, 2.5, 4, 5.5, 7, 7.5)
DIRECT_LAGS = (1, None, 2.5, None, 4, 4.5)


def kernel(inv_hbm, pair_hbm, coef_hbm, out_ref, inv, pair, cstage, ct, cts, part, crecv, zsend, keep, zrecv, gamma, acc,
           local, pair_s, pair_r, core_s, core_r, z_s, z_r, ag_s, ag_r, back_s, back_r):
    rows, here = pair_hbm.shape
    cols = inv_hbm.shape[1]
    basis, virt = coef_hbm.shape
    ticks = virt // TICK
    half_tick, piece = TICK // 2, TICK // 8
    row, col = lax.axis_index("row"), lax.axis_index("col")
    z, core = row // 2, row % 2
    y, x = col // 4, col % 4

    def at_xy(step_x, step_y):
        return (row, (y + step_y) % 4 * 4 + (x + step_x) % 4)

    def at_z(step):
        return ((z + step) % 4 * 2 + core, col)

    sibling = (z * 2 + 1 - core, col)

    def ds(start, size):
        return pl.ds(pl.multiple_of(start, size), size)

    load_pair = pltpu.make_async_copy(pair_hbm, pair.at[pl.ds(0, rows)], local.at[0])
    load_inv = pltpu.make_async_copy(inv_hbm, inv, local.at[1])
    quarter = virt // 4
    load_c = [
        pltpu.make_async_copy(coef_hbm.at[:, pl.ds(k * quarter, quarter)], cstage.at[k % 2], local.at[2 + k]) for k in range(4)
    ]
    load_pair.start()
    load_c[0].start()
    load_c[1].start()
    load_inv.start()

    barrier = pltpu.get_barrier_semaphore()
    for device in (at_xy(1, 0), at_xy(3, 0), at_xy(0, 1), at_xy(0, 3), at_z(1), at_z(2), at_z(3), sibling):
        pl.semaphore_signal(barrier, inc=1, device_id=device, device_id_type=MESH)
    pl.semaphore_wait(barrier, 8)

    def pair_copy(copy):
        source, target, step_x, step_y = copy
        origin = pair_hbm if source < 4 else pair
        size, at = SIZES[source], COPIES.index(copy)
        return pltpu.make_async_remote_copy(
            origin.at[pl.ds(STARTS[source], size)], pair.at[pl.ds(STARTS[target], size)], pair_s.at[at], pair_r.at[at],
            device_id=at_xy(step_x, step_y), device_id_type=MESH,
        )

    own = [copy for slot in range(4) for copy in SENDS[slot]]
    for copy in sorted(own, key=lambda c: ((c[2] != 0) != (c[0] < 2), c[0] % 2)):
        pair_copy(copy).start()

    acc[...] = jnp.zeros_like(acc)
    for k in range(4):
        load_c[k].wait()
        ct[pl.ds(k * quarter, quarter), :] = cstage[k % 2].T
        if k + 2 < 4:
            load_c[k + 2].start()
    for slot, (half, dx, dy, part_of) in enumerate(SLOTS):
        block = (y + dy) % 4 * 4 + (x + dx) % 4
        start = pl.multiple_of(block * rows + half * HALF + PARTS[part_of][0], 16)
        cts[pl.ds(STARTS[slot], SIZES[slot]), :] = ct[pl.ds(start, SIZES[slot]), :]
    load_pair.wait()
    load_inv.wait()

    holds_diag = col // 2 == row
    diag_at = pl.multiple_of(col % 2 * cols, cols)

    def core_copy(u):
        return pltpu.make_async_remote_copy(
            part.at[u % 4, ds((1 - core) * half_tick, half_tick)], crecv.at[ds(u * half_tick, half_tick)],
            core_s.at[u], core_r.at[u], device_id=sibling, device_id_type=MESH,
        )

    ahead = 1 - 2 * core
    steps = (ahead, -ahead, ahead)

    def piece_at(u, step):
        return ds(u * half_tick + (z + step + 4) % 4 * piece, piece)

    def z_send(u, k, step, owner):
        return pltpu.make_async_remote_copy(
            zsend.at[piece_at(u, owner)], zrecv.at[ds((u * 3 + k) * piece, piece)],
            z_s.at[u, k], z_r.at[u, k], device_id=at_z(step + 4), device_id_type=MESH,
        )

    def spread_send(u, k, step, owner):
        rows_of = ds(u * TICK + core * half_tick + (z + owner + 4) % 4 * piece, piece)
        return pltpu.make_async_remote_copy(
            gamma.at[rows_of], gamma.at[rows_of], ag_s.at[u, k], ag_r.at[u, k],
            device_id=at_z(step + 4), device_id_type=MESH,
        )

    def back_copy(u):
        mine = ds(u * TICK + core * half_tick, half_tick)
        return pltpu.make_async_remote_copy(
            gamma.at[mine], gamma.at[mine], back_s.at[u], back_r.at[u], device_id=sibling, device_id_type=MESH,
        )

    def arrive(t):
        for group in GROUPS:
            @pl.when(t == STARTS[group[0]] // TICK)
            def _():
                for slot in group:
                    pair_copy(FILLED[slot]).wait_recv()
                    for copy in SENDS.get(slot, ()):
                        pair_copy(copy).start()

    def product(t):
        @pl.when(t >= 4)
        def _():
            core_copy(t - 4).wait_send()

        now = ds(t * TICK, TICK)
        part[t % 4] = jnp.dot(pair[now, :], inv[...], preferred_element_type=F32)

        @pl.when(holds_diag)
        def _():
            part[t % 4] = part[t % 4] - pair[now, pl.ds(diag_at, cols)].astype(F32)

        core_copy(t).start()

    def add_cores(u, direct):
        core_copy(u).wait_recv()
        total = part[u % 4, ds(core * half_tick, half_tick)] + crecv[ds(u * half_tick, half_tick)]
        zsend[ds(u * half_tick, half_tick)] = total.astype(BF16)
        z_send(u, 0, 2 if direct else ahead, 2).start()
        z_send(u, 1, -ahead, -ahead).start()
        if direct:
            z_send(u, 2, ahead, ahead).start()
        for k, owner in enumerate((0,) if direct else (0, ahead)):
            at = (z + owner + 4) % 4 * piece
            keep[u % 8, pl.ds(k * piece, piece)] = (
                part[u % 4, ds(core * half_tick + at, piece)] + crecv[ds(u * half_tick + at, piece)]
            )

    def relay(u, direct):
        z_send(u, 0, ahead, 2).wait_recv()
        total = keep[u % 8, pl.ds(piece, piece)] + zrecv[ds(u * 3 * piece, piece)].astype(F32)
        zsend[piece_at(u, ahead)] = total.astype(BF16)
        z_send(u, 2, ahead, ahead).start()

    def add_z(u, direct):
        total = keep[u % 8, pl.ds(0, piece)]
        for k in (1, 2, 0) if direct else (1, 2):
            z_send(u, k, steps[k], 0).wait_recv()
            total = total + zrecv[ds((u * 3 + k) * piece, piece)].astype(F32)
        gamma[ds(u * TICK + core * half_tick + z * piece, piece)] = total.astype(BF16)
        if direct:
            spread_send(u, 2, 2, 0).start()
        spread_send(u, 0, ahead, 0).start()
        spread_send(u, 1, -ahead, 0).start()

    def spread_relay(u, direct):
        spread_send(u, 0, ahead, -ahead).wait_recv()
        spread_send(u, 2, ahead, -ahead).start()

    def spread_cores(u, direct):
        if direct:
            spread_send(u, 0, ahead, -ahead).wait_recv()
        spread_send(u, 1, -ahead, ahead).wait_recv()
        spread_send(u, 2, ahead, 2).wait_recv()
        back_copy(u).start()

    def transform(u, direct):
        back_copy(u).wait_recv()

        @pl.when(u % 2 == 1)
        def _():
            now = ds((u - 1) * TICK, 2 * TICK)
            acc[...] += lax.dot_general(gamma[now, :], cts[now, :], (((0,), (0,)), ((), ())), preferred_element_type=F32)

        for k in range(3):
            z_send(u, k, steps[k], 0).wait_send()
            spread_send(u, k, steps[k], 0).wait_send()
        back_copy(u).wait_send()

    stages = (add_cores, relay, add_z, spread_relay, spread_cores, transform)
    turn = ticks - DIRECT
    plan = [(lag, 0, turn, stage, False) for lag, stage in zip(RELAY_LAGS, stages) if turn and lag is not None]
    plan += [(lag, turn, ticks, stage, True) for lag, stage in zip(DIRECT_LAGS, stages) if DIRECT and lag is not None]

    def tick(t, _):
        def run(after):
            for lag, first, last, stage, direct in plan:
                if (lag != int(lag)) == after:
                    @pl.when((t >= int(lag) + first) & (t < int(lag) + last))
                    def _():
                        stage(t - int(lag), direct)

        @pl.when(t < ticks)
        def _():
            arrive(t)

        run(False)

        @pl.when(t < ticks)
        def _():
            product(t)

        run(True)
        return 0

    lax.fori_loop(0, max(int(lag) + last for lag, _, last, _, _ in plan), tick, 0)
    out_ref[...] = acc[...].astype(BF16)
    for copy in COPIES:
        pair_copy(copy).wait_send()
    for u in range(ticks - 4, ticks):
        core_copy(u).wait_send()


def shards(inverse, pair_block, coeffs):
    here, cols = inverse.shape
    rows = pair_block.shape[1]
    basis, virt = coeffs.shape
    ticks = virt // TICK
    dma = pltpu.SemaphoreType.DMA
    any_space = pl.BlockSpec(memory_space=pl.ANY)
    return pl.pallas_call(
        kernel,
        out_shape=jax.ShapeDtypeStruct((cols, basis), BF16),
        in_specs=[any_space] * 3,
        out_specs=pl.BlockSpec(memory_space=pltpu.VMEM),
        scratch_shapes=[
            pltpu.VMEM((here, cols), BF16),
            pltpu.VMEM((virt, here), BF16),
            pltpu.VMEM((2, basis, virt // 4), BF16),
            pltpu.VMEM((virt, basis), BF16),
            pltpu.VMEM((virt, basis), BF16),
            pltpu.VMEM((4, TICK, cols), F32),
            pltpu.VMEM((virt // 2, cols), F32),
            pltpu.VMEM((virt // 2, cols), BF16),
            pltpu.VMEM((8, TICK // 4, cols), F32),
            pltpu.VMEM((ticks * 3 * TICK // 8, cols), BF16),
            pltpu.VMEM((virt, cols), BF16),
            pltpu.VMEM((cols, basis), F32),
            dma((6,)),
            dma((len(COPIES),)), dma((len(COPIES),)),
            dma((ticks,)), dma((ticks,)),
            dma((ticks, 3)), dma((ticks, 3)),
            dma((ticks, 3)), dma((ticks, 3)),
            dma((ticks,)), dma((ticks,)),
        ],
        compiler_params=pltpu.CompilerParams(collective_id=0, has_side_effects=True, vmem_limit_bytes=51 << 20),
    )(inverse, pair_block.T, coeffs)


def solution(mesh):
    placed = (P("row", "col"), P("row", "col"), P("row", None))
    return jax.shard_map(
        shards, mesh=mesh, in_specs=placed, out_specs=P("col", "row"), check_vma=False
    )
```

time: 109 us -> 101 us (0.927)
  Pallas kernels: 106 us -> 98.3 us
    pallas_call x1, Pallas kernels: 106 us -> 98.3 us  [shards(): pl.pallas_call(kernel, out_shape=jax.ShapeDtypeStruct((cols, basis), BF16...]
    unnamed x1 -> x3, local copies, waits for them, and re-layouts: 2.61 us -> 2.23 us
where the time goes in v2:
time: 101 us
  Pallas kernels  98.3 us (97%)
  local copies, waits for them, and re-layouts  2.23 us (2%)
    pallas_call x1, Pallas kernels, shards(): pl.pallas_call(kernel, out_shape=jax.ShapeDtypeStruct((cols, basis), BF16...  98.3 us
    unnamed x3, local copies, waits for them, and re-layouts  2.23 us

profile of v2, /device:TPU:1, one launch (start us, length us, event | category | flops | bytes accessed | tf_op | source)
XLA Modules:
  0.0 100.6 jit_solution(11959593674043362771)
XLA Ops:
  0.0 0.0 copy-start
  0.0 1.1 %copy-done = bf16[2304,160]{0,1:T(8,128)(2,1)S(1)} copy-done((bf16[2304,160]{0,1:T(8,128)(2,1)S(1)}, bf16[2304,160]{0,1:T(8,128)(2,1)}, u32[]{:S(2)}) %copy-start) | copy-done | bytes 737304
  1.1 98.3 %shard_map.37 = bf16[1152,640]{1,0:T(8,128)(2,1)S(1)} custom-call(bf16[2304,1152]{1,0:T(8,128)(2,1)} %inv_hbm.1, bf16[160,2304]{1,0:T(8,128)(2,1)S(1)} %bitcast.1, bf16[640,2560]{1,0:T(8,128)(2,1)} %coef_hbm.1), custom_call_target="tpu_custom_call" | custom-call | tf_op jit(solution)/shard_map/pallas_call | solution.py:299
  99.5 1.1 %copy.5 = bf16[1152,640]{1,0:T(8,128)(2,1)} copy(bf16[1152,640]{1,0:T(8,128)(2,1)S(1)} %shard_map.37) | data formatting | bytes 2949120
Async XLA Ops:
  0.0 1.1 %copy-start = (bf16[2304,160]{0,1:T(8,128)(2,1)S(1)}, bf16[2304,160]{0,1:T(8,128)(2,1)}, u32[]{:S(2)}) copy-start(bf16[2304,160]{0,1:T(8,128)(2,1)} %param.4) | copy-start | bytes 2211844

commit v3 on v2

--- a/solution.py
+++ b/solution.py
@@ -74,7 +74,7 @@
 COPIES = [FILLED[slot] for slot in sorted(FILLED)]
 
 TICK = 128
-DIRECT = 4
+DIRECT = 2
 RELAY_LAGS = (1, 2.5, 4, 5.5, 7, 7.5)
 DIRECT_LAGS = (1, None, 2.5, None, 4, 4.5)
 

time: 101 us -> 99.4 us (0.984)
  Pallas kernels: 98.3 us -> 97 us
    pallas_call x1, Pallas kernels: 98.3 us -> 97 us  [shards(): pl.pallas_call(kernel, out_shape=jax.ShapeDtypeStruct((cols, basis), BF16...]
where the time goes in v3:
time: 99.4 us; the launch traced here: 99.2 us
  Pallas kernels  97 us (98%)
  local copies, waits for them, and re-layouts  2.23 us (2%)
    pallas_call x1, Pallas kernels, shards(): pl.pallas_call(kernel, out_shape=jax.ShapeDtypeStruct((cols, basis), BF16...  97 us
    unnamed x3, local copies, waits for them, and re-layouts  2.23 us

profile of v3, /device:TPU:1, one launch (start us, length us, event | category | flops | bytes accessed | tf_op | source)
XLA Modules:
  0.0 99.2 jit_solution(497028224598565054)
XLA Ops:
  0.0 0.0 copy-start
  0.0 1.1 %copy-done = bf16[2304,160]{0,1:T(8,128)(2,1)S(1)} copy-done((bf16[2304,160]{0,1:T(8,128)(2,1)S(1)}, bf16[2304,160]{0,1:T(8,128)(2,1)}, u32[]{:S(2)}) %copy-start) | copy-done | bytes 737304
  1.1 97.0 %shard_map.37 = bf16[1152,640]{1,0:T(8,128)(2,1)S(1)} custom-call(bf16[2304,1152]{1,0:T(8,128)(2,1)} %inv_hbm.1, bf16[160,2304]{1,0:T(8,128)(2,1)S(1)} %bitcast.1, bf16[640,2560]{1,0:T(8,128)(2,1)} %coef_hbm.1), custom_call_target="tpu_custom_call" | custom-call | tf_op jit(solution)/shard_map/pallas_call | solution.py:299
  98.1 1.1 %copy.5 = bf16[1152,640]{1,0:T(8,128)(2,1)} copy(bf16[1152,640]{1,0:T(8,128)(2,1)S(1)} %shard_map.37) | data formatting | bytes 2949120
Async XLA Ops:
  0.0 1.1 %copy-start = (bf16[2304,160]{0,1:T(8,128)(2,1)S(1)}, bf16[2304,160]{0,1:T(8,128)(2,1)}, u32[]{:S(2)}) copy-start(bf16[2304,160]{0,1:T(8,128)(2,1)} %param.4) | copy-start | bytes 2211844
